TPU v7x, 32 devices: a whole 2x2x4 slice. The times are simulated.
32 devices in a mesh: row: 4 (over y, core), col: 8 (over z, x).
Axes of the slice: x: 2, y: 2, z: 4, core: 2. Of those that a mesh axis runs over, the one named last changes fastest.
Arguments:
- object_field: float32 [2, 1024, 2048], P(None, 'row', 'col'), may hold values from -4 to 4
- modes: bfloat16 [4, 12, 2, 256, 256], P('row', None, None, 'col'), may hold values from -5 to 5
- coeffs: float32 [4, 8, 4, 12], P('row', 'col'), may hold values from -1.5 to 1.5
- offsets: int32 [4, 8, 4, 2], P('row', 'col'), may hold values from -128 to 128, as said below
- region: int32 [4, 8, 4], P('row', 'col'), may hold values from 0 to 3, as said below
- counts: int32 [4, 8], P('row', 'col'), may hold values from 1 to 4, as said below
- intensity: bfloat16 [4, 8, 4, 256, 256], P('row', 'col'), may hold values from 0.049804688 to 4
Outputs:
- object_grad: float32 [2, 1024, 2048], P(None, 'row', 'col')
- mode_grad: float32 [4, 12, 2, 256, 256], P('row', None, None, 'col')
Inputs may be any that keep to these rules, and one draw needn't show every extreme that they name: `offsets`: every window reaches at most 128 cells beyond its tile on each side; every tile has a live slot whose window starts at row offset -128 and column offset 256 - 256 / 2. A position's region is its tile's row index or the next one; slot 0 of every tile has its own row's region. Slots 0 to counts - 1 of a tile are live, the rest are ignored; some tile is full and some tile has one live slot.
All inputs are finite; a program needn't handle non-finite values.
Results may differ from a plain program's by a relative error of at most 0.014.
Values may be sent and summed in bfloat16 or wider, within the bound.
No kernel may reach another device: no remote copies, remote signals or barrier semaphores. Data moves between devices by JAX's collectives and lax.ppermute only.
A program may use at most 64 MiB of HBM per device.

v0:
```python
import math

import jax
import jax.numpy as jnp
from jax import lax
from jax.sharding import PartitionSpec as P

FLOOR = 0.25


def extended_2(x, sides, width):
    for axis, dim in sides:
        size, length = (lax.axis_size(axis), x.shape[dim])
        up = [(i, (i + 1) % size) for i in range(size - 1)]
        down = [(j, i) for i, j in up]
        last = lax.slice_in_dim(x, length - width, length, axis=dim)
        leading = lax.slice_in_dim(x, 0, width, axis=dim)
        before = lax.ppermute(last, axis, up)
        after = lax.ppermute(leading, axis, down)
        x = jnp.concatenate([before, x, after], axis=dim)
    return x


def from_behind(value, axis, steps):
    count = lax.axis_size(axis)
    leading, last = (max(0, -steps), min(count, count - steps))
    return lax.ppermute(value, axis, [(source, source + steps) for source in range(leading, last)])


def dft_tables(length):
    indices = jnp.arange(length, dtype=jnp.int32)
    phases = indices[:, None] * indices[None, :] % length
    angles = phases.astype(jnp.float32) * (2.0 * math.pi / length)
    scaling = 1.0 / math.sqrt(length)
    return (
        (jnp.cos(angles) * scaling).astype(jnp.bfloat16),
        (-jnp.sin(angles) * scaling).astype(jnp.bfloat16),
    )


def left_apply(table_re, table_im, real_part, imag_part, orient):

    def multiply(table, operand):
        return jnp.einsum("mr,prn->pmn", table, operand, preferred_element_type=jnp.float32)

    out_re = multiply(table_re, real_part) - orient * multiply(table_im, imag_part)
    out_im = multiply(table_re, imag_part) + orient * multiply(table_im, real_part)
    return (out_re, out_im)


def right_apply(table_re, table_im, real_part, imag_part, orient):

    def multiply(operand, table):
        return jnp.einsum("pmc,cn->pmn", operand, table, preferred_element_type=jnp.float32)

    out_re = multiply(real_part, table_re) - orient * multiply(imag_part, table_im)
    out_im = multiply(imag_part, table_re) + orient * multiply(real_part, table_im)
    return (out_re, out_im)


def local(object_field, modes, coeffs, offsets, region, counts, intensity):
    window_size = modes.shape[-1]
    half_size = window_size // 2
    num_modes = modes.shape[1]
    slot_count = coeffs.shape[2]
    row_index = lax.axis_index("row")
    object_low = object_field.astype(jnp.bfloat16)
    extended = extended_2(object_low, (("row", 1), ("col", 2)), half_size)
    follower = from_behind(modes, "row", -1)
    stacked = jnp.concatenate([modes[0], follower[0]], axis=0)
    stack_count = stacked.shape[0]
    weights = coeffs[0, 0]
    regions = region[0, 0]
    own_mask = (regions == row_index).astype(jnp.float32)
    next_mask = (regions == row_index + 1).astype(jnp.float32)
    mixing = jnp.concatenate([weights * own_mask[:, None], weights * next_mask[:, None]], axis=1)
    mixing_all = lax.all_gather(mixing, "col", axis=0, tiled=True)
    flattened = stacked.reshape(stack_count, -1).astype(jnp.float32)
    slabs = jnp.dot(
        mixing_all, flattened, precision=lax.Precision.HIGHEST, preferred_element_type=jnp.float32
    )
    slabs = slabs.reshape(mixing_all.shape[0], 2, stacked.shape[2], stacked.shape[3]).astype(
        jnp.bfloat16
    )
    probes = lax.all_to_all(slabs, "col", split_axis=0, concat_axis=2, tiled=True)
    corners = offsets[0, 0]

    def cut_window(corner):
        return lax.dynamic_slice(
            extended,
            (jnp.int32(0), corner[0] + half_size, corner[1] + half_size),
            (2, window_size, window_size),
        )

    windows = jax.vmap(cut_window)(corners)
    probe_re = probes[:, 0].astype(jnp.float32)
    probe_im = probes[:, 1].astype(jnp.float32)
    window_re = windows[:, 0].astype(jnp.float32)
    window_im = windows[:, 1].astype(jnp.float32)
    exit_re = (probe_re * window_re - probe_im * window_im).astype(jnp.bfloat16)
    exit_im = (probe_re * window_im + probe_im * window_re).astype(jnp.bfloat16)
    table_re, table_im = dft_tables(window_size)
    half_re, half_im = left_apply(table_re, table_im, exit_re, exit_im, 1.0)
    far_re, far_im = right_apply(
        table_re, table_im, half_re.astype(jnp.bfloat16), half_im.astype(jnp.bfloat16), 1.0
    )
    magnitude = jnp.sqrt(far_re * far_re + far_im * far_im)
    measured = jnp.sqrt(intensity[0, 0].astype(jnp.float32))
    live = (jnp.arange(slot_count, dtype=jnp.int32) < counts[0, 0]).astype(jnp.float32)
    factor = (measured / jnp.maximum(magnitude, FLOOR) - 1.0) * live[:, None, None]
    change_re = (far_re * factor).astype(jnp.bfloat16)
    change_im = (far_im * factor).astype(jnp.bfloat16)
    back_re, back_im = left_apply(table_re, table_im, change_re, change_im, -1.0)
    update_re, update_im = right_apply(
        table_re, table_im, back_re.astype(jnp.bfloat16), back_im.astype(jnp.bfloat16), -1.0
    )
    object_terms = jnp.stack(
        [probe_re * update_re + probe_im * update_im, probe_re * update_im - probe_im * update_re],
        axis=1,
    )
    terms = jnp.stack(
        [
            window_re * update_re + window_im * update_im,
            window_re * update_im - window_im * update_re,
        ],
        axis=1,
    ).astype(jnp.bfloat16)

    def place(position, accum):
        start_row = corners[position, 0] + half_size
        start_col = corners[position, 1] + half_size
        current = lax.dynamic_slice(
            accum, (jnp.int32(0), start_row, start_col), (2, window_size, window_size)
        )
        return lax.dynamic_update_slice(
            accum, current + object_terms[position], (jnp.int32(0), start_row, start_col)
        )

    accum = lax.fori_loop(0, slot_count, place, jnp.zeros(extended.shape, jnp.float32))
    received = lax.all_to_all(terms, "col", split_axis=2, concat_axis=0, tiled=True)
    col_count = lax.axis_size("col")
    per_source = jnp.einsum(
        "dpk,dpx->dkx",
        mixing_all.reshape(col_count, slot_count, -1),
        received.reshape(col_count, slot_count, -1).astype(jnp.float32),
        precision=lax.Precision.HIGHEST,
        preferred_element_type=jnp.float32,
    )
    rounded = lax.optimization_barrier(per_source.astype(jnp.bfloat16)).astype(jnp.float32)
    summed = jnp.sum(rounded, axis=0).reshape(stack_count, 2, received.shape[2], window_size)
    own_sum = summed[:num_modes]
    passed = from_behind(summed[num_modes:].astype(jnp.bfloat16), "row", 1).astype(jnp.float32)
    mode_grad = (own_sum + passed)[None]
    outer_rows = jnp.concatenate([accum[:, :half_size], accum[:, -half_size:]], axis=1)
    got_rows = extended_2(outer_rows.astype(jnp.bfloat16), (("row", 1),), half_size).astype(
        outer_rows.dtype
    )
    middle = accum[:, half_size:-half_size]
    middle = middle.at[:, :half_size].add(got_rows[:, :half_size])
    middle = middle.at[:, -half_size:].add(got_rows[:, -half_size:])
    outer_cols = jnp.concatenate([middle[:, :, :half_size], middle[:, :, -half_size:]], axis=2)
    got_cols = extended_2(outer_cols.astype(jnp.bfloat16), (("col", 2),), half_size).astype(
        outer_cols.dtype
    )
    object_grad = middle[:, :, half_size:-half_size]
    object_grad = object_grad.at[:, :, :half_size].add(got_cols[:, :, :half_size])
    object_grad = object_grad.at[:, :, -half_size:].add(got_cols[:, :, -half_size:])
    return (object_grad, mode_grad)


def solution(mesh):
    in_specs = (
        P(None, "row", "col"),
        P("row", None, None, "col", None),
        P("row", "col", None, None),
        P("row", "col", None, None),
        P("row", "col", None),
        P("row", "col"),
        P("row", "col", None, None, None),
    )
    out_specs = (P(None, "row", "col"), P("row", None, None, "col", None))
    return jax.shard_map(local, mesh=mesh, in_specs=in_specs, out_specs=out_specs, check_vma=False)
```

profile of v0, /device:TPU:20, one launch (start us, length us, event | category | flops | bytes accessed | tf_op | source)
XLA Modules:
  0.0 194.3 jit_solution(16721502046755920107)
XLA Ops:
  1.7 1.9 collective-permute-start.1
  3.7 3.6 %collective-permute-start.2 = (bf16[2,128,256]{2,1,0:T(8,128)(2,1)S(1)}, bf16[2,128,256]{2,1,0:T(8,128)(2,1)S(1)}, u32[]{:S(2)}, u32[]{:S(2)}) collective-permute-start(bf16[2,128,256]{2,1,0:T(8,128)(2,1)S(1)} %get-tuple-element.244), channel_id=1, source_target_pairs={{8,0},{16,8},{24,16},{9,1},{17,9},{25,17},{10,2},{18,10},{26,18},{... | collective-permute-start | bytes 393224 | tf_op jit(solution)/shard_map/ppermute | solution.py:19
  7.3 1.9 collective-permute-start
  12.0 23.8 %all-gather = f32[8,4,24]{2,1,0:T(4,128)S(1)} all-gather(f32[1,4,24]{2,1,0:T(4,128)S(1)} %maximum_bitcast_fusion), channel_id=1, replica_groups=mesh['row'=4,'col'=8] {'col'}, dimensions={0}, use_global_device_ids=true | all-gather | bytes 3456 | tf_op jit(solution)/shard_map/all_gather | solution.py:77
  36.0 3.4 %collective-permute-start.3 = (bf16[2,512,128]{2,1,0:T(8,128)(2,1)S(1)}, bf16[2,512,128]{2,1,0:T(8,128)(2,1)S(1)}, u32[]{:S(2)}, u32[]{:S(2)}) collective-permute-start(bf16[2,512,128]{2,1,0:T(8,128)(2,1)S(1)} %get-tuple-element.241), channel_id=1, source_target_pairs={{0,1},{1,2},{2,3},{3,4},{4,5},{5,6},{6,7},{8,9},{9,10},{10,11},{11... | collective-permute-start | bytes 786440 | tf_op jit(solution)/shard_map/ppermute | solution.py:18
  39.4 3.3 %collective-permute-start.4 = (bf16[2,512,128]{2,1,0:T(8,128)(2,1)S(1)}, bf16[2,512,128]{2,1,0:T(8,128)(2,1)}, u32[]{:S(2)}, u32[]{:S(2)}) collective-permute-start(bf16[2,512,128]{2,1,0:T(8,128)(2,1)S(1)} %get-tuple-element.242), channel_id=1, source_target_pairs={{1,0},{2,1},{3,2},{4,3},{5,4},{6,5},{7,6},{9,8},{10,9},{11,10},{12... | collective-permute-start | bytes 786440 | tf_op jit(solution)/shard_map/ppermute | solution.py:19
  46.3 6.7 %all-to-all-start = ((bf16[32,2,32,256]{3,2,1,0:T(8,128)(2,1)}), bf16[32,2,32,256]{3,2,1,0:T(8,128)(2,1)S(1)}, u32[]{:S(2)}, u32[]{:S(2)}) async-start(bf16[32,2,32,256]{3,2,1,0:T(8,128)(2,1)} %copy.58), calls=%async_computation | async-start | bytes 2097152 | tf_op jit(solution)/shard_map/all_to_all | solution.py:85
  56.8 11.2 %while.22 = (s32[]{:T(128)}, bf16[2,512,512]{2,1,0:T(8,128)(2,1)S(1)}, s32[4,3]{1,0:T(4,128)}, bf16[4,2,256,256]{3,2,0,1:T(8,128)(2,1)S(1)}, s32[]{:T(128)}) while((s32[]{:T(128)}, bf16[2,512,512]{2,1,0:T(8,128)(2,1)S(1)}, s32[4,3]{1,0:T(4,128)}, bf16[4,2,256,256]{3,2,0,1:T(8,128)(2,1)S(1)}, s32[]{:T(128)}) %tuple.95), condition=%wide.while_cond.4, body=%wide.while_body.4.sunk | while | flops 2 | bytes 524413 | solution.py:89
  68.1 3.9 %all-to-all-done = bf16[32,2,32,256]{3,2,1,0:T(8,128)(2,1)S(1)} async-done(((bf16[32,2,32,256]{3,2,1,0:T(8,128)(2,1)}), bf16[32,2,32,256]{3,2,1,0:T(8,128)(2,1)S(1)}, u32[]{:S(2)}, u32[]{:S(2)}) %all-to-all-start) | async-done | bytes 1048608 | tf_op jit(solution)/shard_map/all_to_all | solution.py:85
  81.3 2.0 %multiply_convert_fusion.1 = (bf16[4,256,256]{2,1,0:T(8,128)(2,1)S(1)}, bf16[4,256,256]{2,1,0:T(8,128)(2,1)S(1)}) fusion(f32[4]{0:T(128)S(1)} %copy-done.7, f32[4,256,256]{2,1,0:T(8,128)S(1)} %convolution_add_fusion, bf16[1,1,4,256,256]{4,3,2,1,0:T(8,128)(2,1)S(1)} %copy-done.6, f32[4,256,256]{2,1,0:T(8,128)S(1)} %fusion.61, bf16[4,256,256]{1,2,0:T(8,128)(2,1)S(1)} %fusion.8), kind=kOutput, calls=%fused_computation.61 | convolution fusion | flops 138739712 | bytes 4194320 | tf_op jit(solution)/shard_map/pmc,cn->pmn/dot_general | solution.py:54
  96.1 7.2 %all-to-all-start.1 = ((bf16[4,2,256,256]{3,0,1,2:T(4,128)(2,1)}), bf16[4,2,256,256]{3,0,1,2:T(4,128)(2,1)}, u32[]{:S(2)}, u32[]{:S(2)}) async-start(bf16[4,2,256,256]{3,0,1,2:T(4,128)(2,1)} %copy.80), calls=%async_computation.1 | async-start | bytes 2097152 | tf_op jit(solution)/shard_map/all_to_all | solution.py:140
  105.6 49.7 %while.21 = (s32[]{:T(128)}, f32[2,512,512]{2,1,0:T(8,128)S(1)}, s32[4,2]{0,1:T(2,128)S(1)}, f32[4,2,256,256]{3,2,0,1:T(8,128)}, s32[]{:T(128)}, /*index=5*/s32[1,1]{0,1:T(1,128)}, s32[]{:T(128)}, s32[1,1]{0,1:T(1,128)}) while((s32[]{:T(128)}, f32[2,512,512]{2,1,0:T(8,128)S(1)}, s32[4,2]{0,1:T(2,128)S(1)}, f32[4,2,256,256]{3,2,0,1:T(8,128)}, ...), condition=%wide.region_1.2_spmd, body=%wide.region_0.1_spmd.sunk | while | flops 131082 | bytes 2621661 | solution.py:139
  110.0 6.0 %dynamic_update_slice.12 = f32[2,512,512]{2,1,0:T(8,128)S(1)} dynamic-update-slice(f32[2,512,512]{2,1,0:T(8,128)S(1)} %get-tuple-element.333, f32[2,256,256]{2,1,0:T(8,128)S(1)} %bitcast_add_fusion.2, s32[]{:T(128)} %constant.199.clone.1..sunk, s32[]{:T(128)S(6)} %select_n.116, s32[]{:T(128)S(6)} %select_n.117) | dynamic-update-slice | bytes 1048580 | tf_op jit(solution)/shard_map/while/body/eval_jaxpr/dynamic_update_slice | solution.py:135
  120.5 8.2 %dynamic_update_slice.12 = f32[2,512,512]{2,1,0:T(8,128)S(1)} dynamic-update-slice(f32[2,512,512]{2,1,0:T(8,128)S(1)} %get-tuple-element.333, f32[2,256,256]{2,1,0:T(8,128)S(1)} %bitcast_add_fusion.2, s32[]{:T(128)} %constant.199.clone.1..sunk, s32[]{:T(128)S(6)} %select_n.116, s32[]{:T(128)S(6)} %select_n.117) | dynamic-update-slice | bytes 1048580 | tf_op jit(solution)/shard_map/while/body/eval_jaxpr/dynamic_update_slice | solution.py:135
  133.2 8.3 %dynamic_update_slice.12 = f32[2,512,512]{2,1,0:T(8,128)S(1)} dynamic-update-slice(f32[2,512,512]{2,1,0:T(8,128)S(1)} %get-tuple-element.333, f32[2,256,256]{2,1,0:T(8,128)S(1)} %bitcast_add_fusion.2, s32[]{:T(128)} %constant.199.clone.1..sunk, s32[]{:T(128)S(6)} %select_n.116, s32[]{:T(128)S(6)} %select_n.117) | dynamic-update-slice | bytes 1048580 | tf_op jit(solution)/shard_map/while/body/eval_jaxpr/dynamic_update_slice | solution.py:135
  146.0 9.3 %dynamic_update_slice.12 = f32[2,512,512]{2,1,0:T(8,128)S(1)} dynamic-update-slice(f32[2,512,512]{2,1,0:T(8,128)S(1)} %get-tuple-element.333, f32[2,256,256]{2,1,0:T(8,128)S(1)} %bitcast_add_fusion.2, s32[]{:T(128)} %constant.199.clone.1..sunk, s32[]{:T(128)S(6)} %select_n.116, s32[]{:T(128)S(6)} %select_n.117) | dynamic-update-slice | bytes 1048580 | tf_op jit(solution)/shard_map/while/body/eval_jaxpr/dynamic_update_slice | solution.py:135
  155.5 2.2 %collective-permute-start.5 = (bf16[2,128,512]{2,1,0:T(8,128)(2,1)S(1)}, bf16[2,128,512]{2,1,0:T(8,128)(2,1)S(1)}, u32[]{:S(2)}, u32[]{:S(2)}) collective-permute-start(bf16[2,128,512]{2,1,0:T(8,128)(2,1)S(1)} %get-tuple-element.237), channel_id=1, source_target_pairs={{0,8},{8,16},{16,24},{1,9},{9,17},{17,25},{2,10},{10,18},{18,26},{... | collective-permute-start | bytes 786440 | tf_op jit(solution)/shard_map/ppermute | solution.py:18
  157.7 3.6 %collective-permute-start.6 = (bf16[2,128,512]{2,1,0:T(8,128)(2,1)S(1)}, bf16[2,128,512]{2,1,0:T(8,128)(2,1)S(1)}, u32[]{:S(2)}, u32[]{:S(2)}) collective-permute-start(bf16[2,128,512]{2,1,0:T(8,128)(2,1)S(1)} %get-tuple-element.238), channel_id=1, source_target_pairs={{8,0},{16,8},{24,16},{9,1},{17,9},{25,17},{10,2},{18,10},{26,18},{... | collective-permute-start | bytes 786440 | tf_op jit(solution)/shard_map/ppermute | solution.py:19
  163.2 2.0 %collective-permute-done.6 = bf16[2,128,512]{2,1,0:T(8,128)(2,1)S(1)} collective-permute-done((bf16[2,128,512]{2,1,0:T(8,128)(2,1)S(1)}, bf16[2,128,512]{2,1,0:T(8,128)(2,1)S(1)}, u32[]{:S(2)}, u32[]{:S(2)}) %collective-permute-start.6) | collective-permute-done | bytes 262176 | tf_op jit(solution)/shard_map/ppermute | solution.py:19
  166.5 2.8 %collective-permute-start.7 = (bf16[2,256,128]{2,1,0:T(8,128)(2,1)S(1)}, bf16[2,256,128]{2,1,0:T(8,128)(2,1)S(1)}, u32[]{:S(2)}, u32[]{:S(2)}) collective-permute-start(bf16[2,256,128]{2,1,0:T(8,128)(2,1)S(1)} %get-tuple-element.239), channel_id=1, source_target_pairs={{0,1},{1,2},{2,3},{3,4},{4,5},{5,6},{6,7},{8,9},{9,10},{10,11},{11... | collective-permute-start | bytes 393224 | tf_op jit(solution)/shard_map/ppermute | solution.py:18
  169.3 6.0 %collective-permute-start.8 = (bf16[2,256,128]{2,1,0:T(8,128)(2,1)S(1)}, bf16[2,256,128]{2,1,0:T(8,128)(2,1)S(1)}, u32[]{:S(2)}, u32[]{:S(2)}) collective-permute-start(bf16[2,256,128]{2,1,0:T(8,128)(2,1)S(1)} %get-tuple-element.240), channel_id=1, source_target_pairs={{1,0},{2,1},{3,2},{4,3},{5,4},{6,5},{7,6},{9,8},{10,9},{11,10},{12... | collective-permute-start | bytes 393224 | tf_op jit(solution)/shard_map/ppermute | solution.py:19
  177.6 5.5 %convolution_convert_fusion = bf16[8,24,16384]{2,1,0:T(8,128)(2,1)S(1)} fusion(f32[8,4,24]{2,1,0:T(4,128)S(1)} %all-gather, bf16[8,4,16384]{2,1,0:T(4,128)(2,1)S(1)} %reshape.183), kind=kOutput, calls=%fused_computation.5 | convolution fusion | flops 154140672 | bytes 7343104 | tf_op jit(solution)/shard_map/dpk,dpx->dkx/dot_general | solution.py:142
  184.2 1.9 collective-permute-start.9
  188.0 5.3 %collective-permute-done.9 = bf16[12,2,32,256]{3,2,1,0:T(8,128)(2,1)S(1)} collective-permute-done((bf16[12,2,32,256]{3,2,1,0:T(8,128)(2,1)S(1)}, bf16[12,2,32,256]{3,2,1,0:T(8,128)(2,1)S(1)}, u32[]{:S(2)}, u32[]{:S(2)}) %collective-permute-start.9) | collective-permute-done | bytes 393248 | tf_op jit(solution)/shard_map/ppermute | solution.py:27
  (106 shorter events, 62.7 us)
Async XLA Ops:
  1.7 34.1 %collective-permute-start.1 = (bf16[2,128,256]{2,1,0:T(8,128)(2,1)S(1)}, bf16[2,128,256]{2,1,0:T(8,128)(2,1)S(1)}, u32[]{:S(2)}, u32[]{:S(2)}) collective-permute-start(bf16[2,128,256]{2,1,0:T(8,128)(2,1)S(1)} %get-tuple-element.243), channel_id=1, source_target_pairs={{0,8},{8,16},{16,24},{1,9},{9,17},{17,25},{2,10},{10,18},{18,26},{... | collective-permute-start | bytes 393224 | tf_op jit(solution)/shard_map/ppermute | solution.py:18
  3.7 32.2 %collective-permute-start.2 = (bf16[2,128,256]{2,1,0:T(8,128)(2,1)S(1)}, bf16[2,128,256]{2,1,0:T(8,128)(2,1)S(1)}, u32[]{:S(2)}, u32[]{:S(2)}) collective-permute-start(bf16[2,128,256]{2,1,0:T(8,128)(2,1)S(1)} %get-tuple-element.244), channel_id=1, source_target_pairs={{8,0},{16,8},{24,16},{9,1},{17,9},{25,17},{10,2},{18,10},{26,18},{... | collective-permute-start | bytes 393224 | tf_op jit(solution)/shard_map/ppermute | solution.py:19
  7.3 35.5 %collective-permute-start = (bf16[1,12,2,32,256]{4,3,2,1,0:T(8,128)(2,1)}, bf16[1,12,2,32,256]{4,3,2,1,0:T(8,128)(2,1)S(1)}, u32[]{:S(2)}, u32[]{:S(2)}) collective-permute-start(bf16[1,12,2,32,256]{4,3,2,1,0:T(8,128)(2,1)} %param.18), channel_id=1, source_target_pairs={{8,0},{16,8},{24,16},{9,1},{17,9},{25,17},{10,2},{18,10},{26,18},{... | collective-permute-start | bytes 1179656 | tf_op jit(solution)/shard_map/ppermute | solution.py:27
  35.8 7.4 %copy-start.2 = (bf16[2,128,256]{2,1,0:T(8,128)(2,1)}, bf16[2,128,256]{2,1,0:T(8,128)(2,1)S(1)}, u32[]{:S(2)}) copy-start(bf16[2,128,256]{2,1,0:T(8,128)(2,1)S(1)} %collective-permute-done.2) | copy-start | bytes 393220
  36.0 18.9 %collective-permute-start.3 = (bf16[2,512,128]{2,1,0:T(8,128)(2,1)S(1)}, bf16[2,512,128]{2,1,0:T(8,128)(2,1)S(1)}, u32[]{:S(2)}, u32[]{:S(2)}) collective-permute-start(bf16[2,512,128]{2,1,0:T(8,128)(2,1)S(1)} %get-tuple-element.241), channel_id=1, source_target_pairs={{0,1},{1,2},{2,3},{3,4},{4,5},{5,6},{6,7},{8,9},{9,10},{10,11},{11... | collective-permute-start | bytes 786440 | tf_op jit(solution)/shard_map/ppermute | solution.py:18
  39.4 16.2 %collective-permute-start.4 = (bf16[2,512,128]{2,1,0:T(8,128)(2,1)S(1)}, bf16[2,512,128]{2,1,0:T(8,128)(2,1)}, u32[]{:S(2)}, u32[]{:S(2)}) collective-permute-start(bf16[2,512,128]{2,1,0:T(8,128)(2,1)S(1)} %get-tuple-element.242), channel_id=1, source_target_pairs={{1,0},{2,1},{3,2},{4,3},{5,4},{6,5},{7,6},{9,8},{10,9},{11,10},{12... | collective-permute-start | bytes 786440 | tf_op jit(solution)/shard_map/ppermute | solution.py:19
  44.7 8.3 %copy-start.4 = (s32[1,1,4,2]{2,3,1,0:T(2,128)S(1)}, s32[1,1,4,2]{2,3,1,0:T(2,128)}, u32[]{:S(2)}) copy-start(s32[1,1,4,2]{2,3,1,0:T(2,128)} %param.20) | copy-start | bytes 100
  46.3 25.7 %all-to-all-start = ((bf16[32,2,32,256]{3,2,1,0:T(8,128)(2,1)}), bf16[32,2,32,256]{3,2,1,0:T(8,128)(2,1)S(1)}, u32[]{:S(2)}, u32[]{:S(2)}) async-start(bf16[32,2,32,256]{3,2,1,0:T(8,128)(2,1)} %copy.58), calls=%async_computation | async-start | bytes 2097152 | tf_op jit(solution)/shard_map/all_to_all | solution.py:85
  54.9 0.7 copy-start.3
  78.8 2.5 %copy-start.6 = (bf16[1,1,4,256,256]{4,3,2,1,0:T(8,128)(2,1)S(1)}, bf16[1,1,4,256,256]{4,3,2,1,0:T(8,128)(2,1)}, u32[]{:S(2)}) copy-start(bf16[1,1,4,256,256]{4,3,2,1,0:T(8,128)(2,1)} %param.23) | copy-start | bytes 1572868
  78.8 2.5 %copy-start.7 = (f32[4]{0:T(128)S(1)}, f32[4]{0:T(128)}, u32[]{:S(2)}) copy-start(f32[4]{0:T(128)} %compare_convert_fusion) | copy-start | bytes 52
  96.1 79.2 %all-to-all-start.1 = ((bf16[4,2,256,256]{3,0,1,2:T(4,128)(2,1)}), bf16[4,2,256,256]{3,0,1,2:T(4,128)(2,1)}, u32[]{:S(2)}, u32[]{:S(2)}) async-start(bf16[4,2,256,256]{3,0,1,2:T(4,128)(2,1)} %copy.80), calls=%async_computation.1 | async-start | bytes 2097152 | tf_op jit(solution)/shard_map/all_to_all | solution.py:140
  104.9 0.7 copy-start.5
  155.5 7.7 %collective-permute-start.5 = (bf16[2,128,512]{2,1,0:T(8,128)(2,1)S(1)}, bf16[2,128,512]{2,1,0:T(8,128)(2,1)S(1)}, u32[]{:S(2)}, u32[]{:S(2)}) collective-permute-start(bf16[2,128,512]{2,1,0:T(8,128)(2,1)S(1)} %get-tuple-element.237), channel_id=1, source_target_pairs={{0,8},{8,16},{16,24},{1,9},{9,17},{17,25},{2,10},{10,18},{18,26},{... | collective-permute-start | bytes 786440 | tf_op jit(solution)/shard_map/ppermute | solution.py:18
  157.7 7.5 %collective-permute-start.6 = (bf16[2,128,512]{2,1,0:T(8,128)(2,1)S(1)}, bf16[2,128,512]{2,1,0:T(8,128)(2,1)S(1)}, u32[]{:S(2)}, u32[]{:S(2)}) collective-permute-start(bf16[2,128,512]{2,1,0:T(8,128)(2,1)S(1)} %get-tuple-element.238), channel_id=1, source_target_pairs={{8,0},{16,8},{24,16},{9,1},{17,9},{25,17},{10,2},{18,10},{26,18},{... | collective-permute-start | bytes 786440 | tf_op jit(solution)/shard_map/ppermute | solution.py:19
  165.4 1.0 copy-start
  166.5 19.6 %collective-permute-start.7 = (bf16[2,256,128]{2,1,0:T(8,128)(2,1)S(1)}, bf16[2,256,128]{2,1,0:T(8,128)(2,1)S(1)}, u32[]{:S(2)}, u32[]{:S(2)}) collective-permute-start(bf16[2,256,128]{2,1,0:T(8,128)(2,1)S(1)} %get-tuple-element.239), channel_id=1, source_target_pairs={{0,1},{1,2},{2,3},{3,4},{4,5},{5,6},{6,7},{8,9},{9,10},{10,11},{11... | collective-permute-start | bytes 393224 | tf_op jit(solution)/shard_map/ppermute | solution.py:18
  169.3 16.8 %collective-permute-start.8 = (bf16[2,256,128]{2,1,0:T(8,128)(2,1)S(1)}, bf16[2,256,128]{2,1,0:T(8,128)(2,1)S(1)}, u32[]{:S(2)}, u32[]{:S(2)}) collective-permute-start(bf16[2,256,128]{2,1,0:T(8,128)(2,1)S(1)} %get-tuple-element.240), channel_id=1, source_target_pairs={{1,0},{2,1},{3,2},{4,3},{5,4},{6,5},{7,6},{9,8},{10,9},{11,10},{12... | collective-permute-start | bytes 393224 | tf_op jit(solution)/shard_map/ppermute | solution.py:19
  184.2 9.1 %collective-permute-start.9 = (bf16[12,2,32,256]{3,2,1,0:T(8,128)(2,1)S(1)}, bf16[12,2,32,256]{3,2,1,0:T(8,128)(2,1)S(1)}, u32[]{:S(2)}, u32[]{:S(2)}) collective-permute-start(bf16[12,2,32,256]{3,2,1,0:T(8,128)(2,1)S(1)} %bitcast.189), channel_id=1, source_target_pairs={{0,8},{8,16},{16,24},{1,9},{9,17},{17,25},{2,10},{10,18},{18,26},{... | collective-permute-start | bytes 1179656 | tf_op jit(solution)/shard_map/ppermute | solution.py:27
  187.2 0.8 copy-start.1
where the time goes:
time: 196 us; the launch traced here: 194 us
  local copies, waits for them, and re-layouts  56.9 us (29%)
  starting transfers between devices  44.7 us (23%)
  matrix products  28.3 us (14%)
  blocking collectives  23.8 us (12%)
  other arithmetic  15 us (8%)
  waiting for transfers between devices  13 us (7%)
  loops' own time  10.8 us (6%)
    dynamic_update_slice x4, local copies, waits for them, and re-layouts, place(): lax.dynamic_update_slice(accum, current + object_terms[position], (jnp.in...  31.8 us
    all_gather x1, blocking collectives, local(): mixing_all = lax.all_gather(mixing, 'col', axis=0, tiled=True)  23.8 us
    ppermute x4, starting transfers between devices, extended_2(): after = lax.ppermute(leading, axis, down)  16.6 us
    dot_general x8, matrix products, multiply(): jnp.einsum('pmc,cn->pmn', operand, table, preferred_element_type=jnp.floa...  11.4 us
    gather x12, local copies, waits for them, and re-layouts  11 us
    another operation x1, loops' own time, local(): lax.fori_loop(0, slot_count, place, jnp.zeros(extended.shape, jnp.float32))  10.5 us
    ppermute x4, starting transfers between devices, extended_2(): before = lax.ppermute(last, axis, up)  10.3 us
    dot_general x8, matrix products, multiply(): jnp.einsum('mr,prn->pmn', table, operand, preferred_element_type=jnp.floa...  10.2 us
  transfers between devices with their start and end apart: 12, of which 4 were waited for; matrix products, arithmetic and copies ran while one was open for 37% of the time, Pallas kernels for 0%

commit v1 on v0

v1 whole, which is shorter than its diff:
```python
import functools
import math

import jax
import jax.numpy as jnp
import numpy as np
from jax import lax
from jax.experimental import pallas as pl
from jax.experimental.pallas import tpu as pltpu
from jax.sharding import PartitionSpec as P

FLOOR = 0.25
LANES = 128
SUBLANES = 8

VMEM = pl.BlockSpec(memory_space=pltpu.VMEM)
SMEM = pl.BlockSpec(memory_space=pltpu.SMEM)


def shift(value, axis, steps):
    count = lax.axis_size(axis)
    leading, last = (max(0, -steps), min(count, count - steps))
    return lax.ppermute(value, axis, [(source, source + steps) for source in range(leading, last)])


def dft_tables(length):
    indices = np.arange(length)
    phases = indices[:, None] * indices[None, :] % length
    angles = phases * (2.0 * math.pi / length)
    scaling = 1.0 / math.sqrt(length)
    re = (np.cos(angles) * scaling).astype(np.float32)
    im = (-np.sin(angles) * scaling).astype(np.float32)
    forward = np.block([[re, -im], [im, re]])
    inverse = np.block([[re, im], [-im, re]])
    return jnp.asarray(forward, jnp.bfloat16), jnp.asarray(inverse, jnp.bfloat16)


def gather_weights(payload, axis):
    count = lax.axis_size(axis)
    if count & (count - 1):
        return lax.all_gather(payload, axis, axis=0, tiled=True)
    mine = lax.broadcasted_iota(jnp.int32, (count, 1), 0) == lax.axis_index(axis)
    state = jnp.where(mine, payload, 0.0)
    step = 1
    while step < count:
        state = state + lax.ppermute(state, axis, [(i, i ^ step) for i in range(count)])
        step *= 2
    return state


def slab_kernel(slots, slot_count, weights, own, follower, out, table):
    num_modes = own.shape[1]
    devices = out.shape[0]
    table[0] = own[0].astype(jnp.float32)
    if follower is not None:
        table[1] = follower[0].astype(jnp.float32)

    def device_step(device, carry):
        for at, slot in enumerate(slots):
            if follower is None:
                which = 0
            else:
                which = jnp.where(weights[device, slot_count * num_modes + slot] > 0.5, 1, 0)
            for part in range(2):
                total = weights[device, slot * num_modes] * table[which, 0, part]
                for k in range(1, num_modes):
                    total += weights[device, slot * num_modes + k] * table[which, k, part]
                out[device, at, part] = total.astype(jnp.bfloat16)
        return carry

    lax.fori_loop(0, devices, device_step, 0)


def slabs(slots, slot_count, weights, own, follower):
    devices = weights.shape[0]
    shape = (devices, len(slots)) + own.shape[2:]
    if follower is None:

        def body(weights, own, out, table):
            slab_kernel(slots, slot_count, weights, own, None, out, table)

        operands, regions = ((weights, own), 1)
    else:
        body = functools.partial(slab_kernel, slots, slot_count)
        operands, regions = ((weights, own, follower), 2)
    return pl.pallas_call(
        body,
        out_shape=jax.ShapeDtypeStruct(shape, jnp.bfloat16),
        in_specs=[SMEM] + [VMEM] * (len(operands) - 1),
        out_specs=VMEM,
        scratch_shapes=[pltpu.VMEM((regions,) + own.shape[1:], jnp.float32)],
        name="slabs",
    )(*operands)


def corner_of(corners, slot, half, limit):
    row = jnp.clip(corners[slot, 0] + half, 0, limit)
    col = jnp.clip(corners[slot, 1] + half, 0, limit)
    rest_row, rest_col = (row & (SUBLANES - 1), col & (LANES - 1))
    base_row = pl.multiple_of(row - rest_row, SUBLANES)
    base_col = pl.multiple_of(col - rest_col, LANES)
    return base_row, rest_row, base_col, rest_col


def window_kernel(corners, tile, left, right, top, bottom, intensity, out, measured, ext):
    size = out.shape[-1]
    half = left.shape[-1]
    rows, cols = tile.shape[1:]
    for part in range(2):
        ext[part, :half, : cols + 2 * half] = top[part].astype(jnp.float32)
        ext[part, half : half + rows, :half] = left[part].astype(jnp.float32)
        ext[part, half : half + rows, half : half + cols] = tile[part].astype(jnp.float32)
        ext[part, half : half + rows, half + cols : cols + 2 * half] = right[part].astype(jnp.float32)
        ext[part, half + rows : 2 * half + rows, : cols + 2 * half] = bottom[part].astype(jnp.float32)
    tall = size + SUBLANES
    wide = size + LANES

    def slot_step(slot, carry):
        base_row, rest_row, base_col, rest_col = corner_of(
            corners, slot, half, rows + 2 * half - size
        )
        for part in range(2):
            block = ext[part, pl.ds(base_row, tall), pl.ds(base_col, wide)]
            block = pltpu.roll(block, lax.rem(tall - rest_row, tall), 0)[:size]
            block = pltpu.roll(block, lax.rem(wide - rest_col, wide), 1)[:, :size]
            out[slot, part] = block.astype(jnp.bfloat16)
        measured[slot] = jnp.sqrt(intensity[0, 0, slot].astype(jnp.float32))
        return carry

    lax.fori_loop(0, out.shape[0], slot_step, 0)


def windows_of(corners, tile, left, right, top, bottom, intensity):
    slot_count = corners.shape[0]
    size = intensity.shape[-1]
    half = left.shape[-1]
    extent = (2, tile.shape[1] + 2 * half + SUBLANES, tile.shape[2] + 2 * half + LANES)
    return pl.pallas_call(
        window_kernel,
        out_shape=(
            jax.ShapeDtypeStruct((slot_count, 2, size, size), jnp.bfloat16),
            jax.ShapeDtypeStruct((slot_count, size, size), jnp.float32),
        ),
        in_specs=[SMEM] + [VMEM] * 6,
        out_specs=(VMEM, VMEM),
        scratch_shapes=[pltpu.VMEM(extent, jnp.float32)],
        name="windows",
    )(corners, tile, left, right, top, bottom, intensity)


def dft_kernel(slots, counts, probes, windows, measured, forward, inverse, terms, placed):
    size = windows.shape[-1]
    devices = probes.shape[0]

    def joined(ref, at, part):
        return ref[:, at, part].reshape(size, size).astype(jnp.float32)

    def dot(left, right):
        return jnp.dot(left, right, preferred_element_type=jnp.float32)

    for at, slot in enumerate(slots):
        probe_re, probe_im = (joined(probes, at, 0), joined(probes, at, 1))
        window_re = windows[slot, 0].astype(jnp.float32)
        window_im = windows[slot, 1].astype(jnp.float32)
        leaving = jnp.concatenate(
            [
                (probe_re * window_re - probe_im * window_im).astype(jnp.bfloat16),
                (probe_re * window_im + probe_im * window_re).astype(jnp.bfloat16),
            ],
            axis=0,
        )
        half = dot(forward[...], leaving).astype(jnp.bfloat16)
        far = dot(jnp.concatenate([half[:size], half[size:]], axis=1), inverse[...])
        far_re, far_im = (far[:, :size], far[:, size:])
        power = jnp.maximum(far_re * far_re + far_im * far_im, FLOOR * FLOOR)
        live = jnp.where(slot < counts[0, 0], 1.0, 0.0).astype(jnp.float32)
        factor = (measured[slot] * lax.rsqrt(power) - 1.0) * live
        change = jnp.concatenate(
            [(far_re * factor).astype(jnp.bfloat16), (far_im * factor).astype(jnp.bfloat16)], axis=0
        )
        back = dot(inverse[...], change).astype(jnp.bfloat16)
        update = dot(jnp.concatenate([back[:size], back[size:]], axis=1), forward[...])
        update_re, update_im = (update[:, :size], update[:, size:])
        blocks = (devices, size // devices, size)
        terms[:, at, 0] = (
            (window_re * update_re + window_im * update_im).astype(jnp.bfloat16).reshape(blocks)
        )
        terms[:, at, 1] = (
            (window_re * update_im - window_im * update_re).astype(jnp.bfloat16).reshape(blocks)
        )
        placed[at, 0] = probe_re * update_re + probe_im * update_im
        placed[at, 1] = probe_re * update_im - probe_im * update_re


def dft_step(slots, counts, probes, windows, measured, tables):
    size = windows.shape[-1]
    return pl.pallas_call(
        functools.partial(dft_kernel, slots),
        out_shape=(
            jax.ShapeDtypeStruct(probes.shape, jnp.bfloat16),
            jax.ShapeDtypeStruct((len(slots), 2, size, size), jnp.float32),
        ),
        in_specs=[SMEM] + [VMEM] * 5,
        out_specs=(VMEM, VMEM),
        name="dft_chain",
    )(counts, probes, windows, measured, *tables)


def place_kernel(groups, half, corners, *refs):
    pieces = refs[: len(groups)]
    top, middle, bottom, accum = refs[len(groups) :]
    size = pieces[0].shape[-1]
    rows = middle.shape[1]
    width = middle.shape[2]
    accum[...] = jnp.zeros_like(accum)
    for slots, piece in zip(groups, pieces):
        for at, slot in enumerate(slots):
            base_row, rest_row, base_col, rest_col = corner_of(
                corners, slot, half, rows + 2 * half - size
            )
            for part in range(2):
                block = jnp.concatenate(
                    [piece[at, part], jnp.zeros((size, LANES), jnp.float32)], axis=1
                )
                block = pltpu.roll(block, rest_col, 1)
                block = jnp.concatenate(
                    [block, jnp.zeros((SUBLANES, size + LANES), jnp.float32)], axis=0
                )
                block = pltpu.roll(block, rest_row, 0)
                where = (part, pl.ds(base_row, size + SUBLANES), pl.ds(base_col, size + LANES))
                accum[where] += block
    top[...] = accum[:, :half, :width].astype(jnp.bfloat16)
    middle[...] = accum[:, half : half + rows, :width]
    bottom[...] = accum[:, half + rows : 2 * half + rows, :width].astype(jnp.bfloat16)


def place(groups, corners, pieces, rows, cols):
    half = pieces[0].shape[-1] // 2
    width = cols + 2 * half
    return pl.pallas_call(
        functools.partial(place_kernel, groups, half),
        out_shape=(
            jax.ShapeDtypeStruct((2, half, width), jnp.bfloat16),
            jax.ShapeDtypeStruct((2, rows, width), jnp.float32),
            jax.ShapeDtypeStruct((2, half, width), jnp.bfloat16),
        ),
        in_specs=[SMEM] + [VMEM] * len(pieces),
        out_specs=(VMEM, VMEM, VMEM),
        scratch_shapes=[
            pltpu.VMEM((2, rows + 2 * half + SUBLANES, width + LANES), jnp.float32)
        ],
        name="place",
    )(corners, *pieces)


def sums_kernel(slots, slot_count, weights, received, own, following, terms):
    num_modes = own.shape[0]
    devices = received.shape[0]
    flags = slot_count * num_modes
    for at in range(len(slots)):
        terms[:, at] = received[:, at].astype(jnp.float32)

    def mode_step(k, carry):
        for part in range(2):
            totals = [jnp.zeros(own.shape[2:], jnp.float32) for _ in range(2)]
            for device in range(devices):
                for at, slot in enumerate(slots):
                    weight = weights[device, slot * num_modes + k]
                    is_next = weights[device, flags + slot]
                    term = terms[device, at, part]
                    totals[0] += (weight * (1.0 - is_next)) * term
                    totals[1] += (weight * is_next) * term
            own[k, part] = totals[0]
            following[k, part] = totals[1].astype(jnp.bfloat16)
        return carry

    lax.fori_loop(0, num_modes, mode_step, 0)


def sums(slots, slot_count, num_modes, weights, received):
    shape = (num_modes,) + received.shape[2:]
    return pl.pallas_call(
        functools.partial(sums_kernel, slots, slot_count),
        out_shape=(
            jax.ShapeDtypeStruct(shape, jnp.float32),
            jax.ShapeDtypeStruct(shape, jnp.bfloat16),
        ),
        in_specs=[SMEM, VMEM],
        out_specs=(VMEM, VMEM),
        scratch_shapes=[pltpu.VMEM(received.shape, jnp.float32)],
        name="mode_sums",
    )(weights, received)


def last_kernel(slots, weights, received, own, passed, out):
    num_modes = own.shape[0]
    devices = received.shape[0]

    def mode_step(k, carry):
        for part in range(2):
            total = own[k, part] + passed[k, part].astype(jnp.float32)
            for device in range(devices):
                for at, slot in enumerate(slots):
                    weight = weights[device, slot * num_modes + k]
                    total += weight * received[device, at, part].astype(jnp.float32)
            out[0, k, part] = total
        return carry

    lax.fori_loop(0, num_modes, mode_step, 0)


def last_sums(slots, weights, received, own, passed):
    return pl.pallas_call(
        functools.partial(last_kernel, slots),
        out_shape=jax.ShapeDtypeStruct((1,) + own.shape, jnp.float32),
        in_specs=[SMEM] + [VMEM] * 3,
        out_specs=VMEM,
        name="last_sums",
    )(weights, received, own, passed)


def local(object_field, modes, coeffs, offsets, region, counts, intensity):
    size = modes.shape[-1]
    half = size // 2
    num_modes = modes.shape[1]
    slot_count = coeffs.shape[2]
    rows, cols = object_field.shape[1:]
    row_index = lax.axis_index("row")

    follower = shift(modes, "row", -1)
    is_own = region[0, 0] == row_index
    is_next = region[0, 0] == row_index + 1
    scaled = coeffs[0, 0] * (is_own | is_next).astype(jnp.float32)[:, None]
    payload = jnp.concatenate([scaled.reshape(-1), is_next.astype(jnp.float32)])
    padding = -payload.shape[0] % LANES
    payload = jnp.pad(payload, (0, padding))[None]
    weights = gather_weights(payload, "col")

    low = object_field.astype(jnp.bfloat16)
    left = shift(low[:, :, cols - half :], "col", 1)
    right = shift(low[:, :, :half], "col", -1)
    wide_top = jnp.concatenate([left[:, :half], low[:, :half], right[:, :half]], axis=2)
    wide_bottom = jnp.concatenate(
        [left[:, rows - half :], low[:, rows - half :], right[:, rows - half :]], axis=2
    )
    top = shift(wide_bottom, "row", 1)
    bottom = shift(wide_top, "row", -1)

    def exchange(value):
        return lax.all_to_all(value, "col", split_axis=0, concat_axis=0, tiled=True)

    first = tuple(range(1, slot_count))
    second = (0,)
    corners = offsets[0, 0]
    tables = dft_tables(size)
    probes_first = exchange(slabs(first, slot_count, weights, modes, follower))
    probes_second = exchange(slabs(second, slot_count, weights, modes, None))
    windows, measured = windows_of(corners, low, left, right, top, bottom, intensity)
    terms_first, placed_first = dft_step(first, counts, probes_first, windows, measured, tables)
    terms_first = exchange(terms_first)
    terms_second, placed_second = dft_step(second, counts, probes_second, windows, measured, tables)
    terms_second = exchange(terms_second)

    over_top, middle, over_bottom = place(
        (first, second), corners, (placed_first, placed_second), rows, cols
    )
    got_top = shift(over_bottom, "row", 1)
    got_bottom = shift(over_top, "row", -1)
    middle = middle.at[:, :half].add(got_top.astype(jnp.float32))
    middle = middle.at[:, rows - half :].add(got_bottom.astype(jnp.float32))
    got_left = shift(middle[:, :, half + cols :].astype(jnp.bfloat16), "col", 1)
    got_right = shift(middle[:, :, :half].astype(jnp.bfloat16), "col", -1)
    object_grad = middle[:, :, half : half + cols]
    object_grad = object_grad.at[:, :, :half].add(got_left.astype(jnp.float32))
    object_grad = object_grad.at[:, :, cols - half :].add(got_right.astype(jnp.float32))

    own, following = sums(first, slot_count, num_modes, weights, terms_first)
    passed = shift(following, "row", 1)
    mode_grad = last_sums(second, weights, terms_second, own, passed)
    return (object_grad, mode_grad)


def solution(mesh):
    in_specs = (
        P(None, "row", "col"),
        P("row", None, None, "col", None),
        P("row", "col", None, None),
        P("row", "col", None, None),
        P("row", "col", None),
        P("row", "col"),
        P("row", "col", None, None, None),
    )
    out_specs = (P(None, "row", "col"), P("row", None, None, "col", None))
    return jax.shard_map(local, mesh=mesh, in_specs=in_specs, out_specs=out_specs, check_vma=False)
```

time: 196 us -> 130 us (0.66)
  local copies, waits for them, and re-layouts: 56.9 us -> 4.02 us
  Pallas kernels: 0 us -> 34.8 us
  matrix products: 28.3 us -> 0 us
  blocking collectives: 23.8 us -> 0 us
  waiting for transfers between devices: 13 us -> 28.1 us
  loops' own time: 10.8 us -> 0 us
  starting transfers between devices: 44.7 us -> 53.4 us
  other arithmetic: 15 us -> 7 us
    pallas_call x0 -> x8, Pallas kernels: none -> 34.8 us  [the longest x2 11.2 us: dft_step(): pl.pallas_call(functools.partial(dft_kernel, slots), out_shape=(jax.Shape...]
    dynamic_update_slice x4 -> x0, local copies, waits for them, and re-layouts: 31.8 us -> none  [place(): lax.dynamic_update_slice(accum, current + object_terms[position], (jnp.in...]
    dot_general x18 -> x0, matrix products: 28.3 us -> none  [the longest x8 11.4 us: multiply(): jnp.einsum('pmc,cn->pmn', operand, table, preferred_element_type=jnp.floa...]
    all_gather x1 -> x0, blocking collectives: 23.8 us -> none  [local(): mixing_all = lax.all_gather(mixing, 'col', axis=0, tiled=True)]
    ppermute x10 -> x13, waiting for transfers between devices: 9.06 us -> 28.1 us  [the longest x10 21.7 us: shift(): lax.ppermute(value, axis, [(source, source + steps) for source in range(l...]
    gather x12 -> x0, local copies, waits for them, and re-layouts: 11 us -> none
    another operation x2 -> x0, loops' own time: 10.8 us -> none  [the longest x1 10.5 us: local(): lax.fori_loop(0, slot_count, place, jnp.zeros(extended.shape, jnp.float32))]
    all_to_all x2 -> x4, starting transfers between devices: 13.9 us -> 21.6 us  [exchange(): return lax.all_to_all(value, 'col', split_axis=0, concat_axis=0, tiled=True)]
  transfers between devices with their start and end apart: 12 -> 17, of which waited for: 4 -> 9; matrix products, arithmetic and copies ran while one was open for 37% -> 5% of each run, Pallas kernels for 0% -> 22%
where the time goes in v1:
time: 130 us; the launch traced here: 129 us
  starting transfers between devices  53.4 us (41%)
  Pallas kernels  34.8 us (27%)
  waiting for transfers between devices  28.1 us (22%)
  other arithmetic  7 us (5%)
  local copies, waits for them, and re-layouts  4.02 us (3%)
  between operations  1.59 us (1%)
    ppermute x10, starting transfers between devices, shift(): lax.ppermute(value, axis, [(source, source + steps) for source in range(l...  28.4 us
    ppermute x10, waiting for transfers between devices, shift(): lax.ppermute(value, axis, [(source, source + steps) for source in range(l...  21.7 us
    all_to_all x4, starting transfers between devices, exchange(): return lax.all_to_all(value, 'col', split_axis=0, concat_axis=0, tiled=True)  21.6 us
    pallas_call x2, Pallas kernels, dft_step(): pl.pallas_call(functools.partial(dft_kernel, slots), out_shape=(jax.Shape...  11.2 us
    ppermute x3, waiting for transfers between devices, gather_weights(): lax.ppermute(state, axis, [(i, i ^ step) for i in range(count)])  6.4 us
    pallas_call x2, Pallas kernels, slabs(): pl.pallas_call(body, out_shape=jax.ShapeDtypeStruct(shape, jnp.bfloat16),...  5.74 us
    pallas_call x1, Pallas kernels, sums(): pl.pallas_call(functools.partial(sums_kernel, slots, slot_count), out_sha...  5.31 us
    pallas_call x1, Pallas kernels, place(): pl.pallas_call(functools.partial(place_kernel, groups, half), out_shape=(...  4.91 us
  transfers between devices with their start and end apart: 17, of which 9 were waited for; matrix products, arithmetic and copies ran while one was open for 5% of the time, Pallas kernels for 22%

profile of v1, /device:TPU:20, one launch (start us, length us, event | category | flops | bytes accessed | tf_op | source)
XLA Modules:
  0.0 128.9 jit_solution(2167773768327609903)
XLA Ops:
  7.6 2.0 %collective-permute-done.1 = f32[8,128]{1,0:T(8,128)S(1)} collective-permute-done((f32[8,128]{1,0:T(8,128)S(1)}, f32[8,128]{1,0:T(8,128)S(1)}, u32[]{:S(2)}, u32[]{:S(2)}) %collective-permute-start.1) | collective-permute-done | bytes 4128 | tf_op jit(solution)/shard_map/ppermute | solution.py:46
  10.1 4.2 %collective-permute-done.2 = f32[8,128]{1,0:T(8,128)S(1)} collective-permute-done((f32[8,128]{1,0:T(8,128)S(1)}, f32[8,128]{1,0:T(8,128)S(1)}, u32[]{:S(2)}, u32[]{:S(2)}) %collective-permute-start.2) | collective-permute-done | bytes 4128 | tf_op jit(solution)/shard_map/ppermute | solution.py:46
  15.6 3.5 %slabs.2 = bf16[8,3,2,32,256]{4,3,2,1,0:T(8,128)(2,1)} custom-call(f32[8,128]{1,0:T(8,128)} %add.45.weights, bf16[1,12,2,32,256]{4,3,2,1,0:T(8,128)(2,1)} %own.3, bf16[1,12,2,32,256]{4,3,2,1,0:T(8,128)(2,1)} %copy-done.10), custom_call_target="tpu_custom_call" | custom-call | tf_op jit(solution)/shard_map/slabs/pallas_call | solution.py:86
  19.1 6.1 %all-to-all-start = ((bf16[8,3,2,32,256]{4,3,2,1,0:T(8,128)(2,1)}), bf16[8,3,2,32,256]{4,3,2,1,0:T(8,128)(2,1)S(1)}, u32[]{:S(2)}, u32[]{:S(2)}) async-start(bf16[8,3,2,32,256]{4,3,2,1,0:T(8,128)(2,1)} %slabs.2), calls=%async_computation | async-start | bytes 1572864 | tf_op jit(solution)/shard_map/all_to_all | solution.py:350
  25.3 3.4 %collective-permute-start.4 = (bf16[2,256,128]{2,1,0:T(8,128)(2,1)S(1)}, bf16[2,256,128]{2,1,0:T(8,128)(2,1)S(1)}, u32[]{:S(2)}, u32[]{:S(2)}) collective-permute-start(bf16[2,256,128]{2,1,0:T(8,128)(2,1)S(1)} %get-tuple-element.77), channel_id=1, source_target_pairs={{0,1},{1,2},{2,3},{3,4},{4,5},{5,6},{6,7},{8,9},{9,10},{10,11},{11... | collective-permute-start | bytes 393224 | tf_op jit(solution)/shard_map/ppermute | solution.py:23
  28.7 3.4 %collective-permute-start.5 = (bf16[2,256,128]{2,1,0:T(8,128)(2,1)S(1)}, bf16[2,256,128]{2,1,0:T(8,128)(2,1)S(1)}, u32[]{:S(2)}, u32[]{:S(2)}) collective-permute-start(bf16[2,256,128]{2,1,0:T(8,128)(2,1)S(1)} %get-tuple-element.76), channel_id=1, source_target_pairs={{1,0},{2,1},{3,2},{4,3},{5,4},{6,5},{7,6},{9,8},{10,9},{11,10},{12... | collective-permute-start | bytes 393224 | tf_op jit(solution)/shard_map/ppermute | solution.py:23
  32.1 2.3 %slabs.3 = bf16[8,1,2,32,256]{4,3,2,1,0:T(8,128)(2,1)} custom-call(f32[8,128]{1,0:T(8,128)} %add.45.weights, bf16[1,12,2,32,256]{4,3,2,1,0:T(8,128)(2,1)} %own.3), custom_call_target="tpu_custom_call" | custom-call | tf_op jit(solution)/shard_map/slabs/pallas_call | solution.py:86
  34.4 7.8 %collective-permute-done.5.right = bf16[2,256,128]{2,1,0:T(8,128)(2,1)S(1)} collective-permute-done((bf16[2,256,128]{2,1,0:T(8,128)(2,1)S(1)}, bf16[2,256,128]{2,1,0:T(8,128)(2,1)S(1)}, u32[]{:S(2)}, u32[]{:S(2)}) %collective-permute-start.5) | collective-permute-done | bytes 131104 | tf_op jit(solution)/shard_map/ppermute | solution.py:23
  44.0 4.3 %all-to-all-start.1 = ((bf16[8,1,2,32,256]{4,3,2,1,0:T(8,128)(2,1)}), bf16[8,1,2,32,256]{4,3,2,1,0:T(8,128)(2,1)S(1)}, u32[]{:S(2)}, u32[]{:S(2)}) async-start(bf16[8,1,2,32,256]{4,3,2,1,0:T(8,128)(2,1)} %slabs.3), calls=%async_computation.1 | async-start | bytes 524288 | tf_op jit(solution)/shard_map/all_to_all | solution.py:350
  50.4 3.6 %collective-permute-start.7 = (bf16[2,128,512]{2,1,0:T(8,128)(2,1)S(1)}, bf16[2,128,512]{2,1,0:T(8,128)(2,1)S(1)}, u32[]{:S(2)}, u32[]{:S(2)}) collective-permute-start(bf16[2,128,512]{2,1,0:T(8,128)(2,1)S(1)} %pad_maximum_fusion.1), channel_id=1, source_target_pairs={{8,0},{16,8},{24,16},{9,1},{17,9},{25,17},{10,2},{18,10},{26,18},{... | collective-permute-start | bytes 786440 | tf_op jit(solution)/shard_map/ppermute | solution.py:23
  58.6 4.6 %windows.1 = (bf16[4,2,256,256]{3,2,1,0:T(8,128)(2,1)}, f32[4,256,256]{2,1,0:T(8,128)}) custom-call(s32[4,2]{1,0:T(4,128)} %copy.12.corners, bf16[2,256,256]{2,1,0:T(8,128)(2,1)} %copy-done.1, bf16[2,256,128]{2,1,0:T(8,128)(2,1)} %copy-done.7, bf16[2,256,128]{2,1,0:T(8,128)(2,1)} %copy-done.8, bf16[2,128,512]{2,1,0:T(8,128)(2,1)} %copy-done.12, ...), custom_call_target="tpu_custom_call" | custom-call | tf_op jit(solution)/shard_map/windows/pallas_call | solution.py:138
  63.2 7.0 %dft_chain.2 = (bf16[8,3,2,32,256]{4,3,2,1,0:T(8,128)(2,1)}, f32[3,2,256,256]{3,2,1,0:T(8,128)}) custom-call(s32[1,1]{1,0:T(1,128)S(6)} %copy.17.counts, bf16[8,3,2,32,256]{4,3,2,1,0:T(8,128)(2,1)} %copy-done.3, bf16[4,2,256,256]{3,2,1,0:T(8,128)(2,1)} %get-tuple-element.61.windows, f32[4,256,256]{2,1,0:T(8,128)} %get-tuple-element.62.measured, ...), custom_call_target="tpu_custom_call" | custom-call | tf_op jit(solution)/shard_map/dft_chain/pallas_call | solution.py:197
  70.2 6.0 %all-to-all-start.3 = ((bf16[8,3,2,32,256]{4,3,2,1,0:T(8,128)(2,1)}), bf16[8,3,2,32,256]{4,3,2,1,0:T(8,128)(2,1)S(1)}, u32[]{:S(2)}, u32[]{:S(2)}) async-start(bf16[8,3,2,32,256]{4,3,2,1,0:T(8,128)(2,1)} %get-tuple-element.69), calls=%async_computation.3 | async-start | bytes 1572864 | tf_op jit(solution)/shard_map/all_to_all | solution.py:350
  76.3 4.2 %dft_chain.3 = (bf16[8,1,2,32,256]{4,3,2,1,0:T(8,128)(2,1)}, f32[1,2,256,256]{3,2,1,0:T(8,128)}) custom-call(s32[1,1]{1,0:T(1,128)S(6)} %copy.17.counts, bf16[8,1,2,32,256]{4,3,2,1,0:T(8,128)(2,1)} %copy-done.5, bf16[4,2,256,256]{3,2,1,0:T(8,128)(2,1)} %get-tuple-element.61.windows, f32[4,256,256]{2,1,0:T(8,128)} %get-tuple-element.62.measured, ...), custom_call_target="tpu_custom_call" | custom-call | tf_op jit(solution)/shard_map/dft_chain/pallas_call | solution.py:197
  80.5 4.9 %place.1 = (bf16[2,128,512]{2,1,0:T(8,128)(2,1)}, f32[2,256,512]{2,1,0:T(8,128)}, bf16[2,128,512]{2,1,0:T(8,128)(2,1)}) custom-call(s32[4,2]{1,0:T(4,128)} %copy.12.corners, f32[3,2,256,256]{3,2,1,0:T(8,128)} %get-tuple-element.63.refs_0_, f32[1,2,256,256]{3,2,1,0:T(8,128)} %get-tuple-element.64.refs_1_), custom_call_target="tpu_custom_call" | custom-call | tf_op jit(solution)/shard_map/place/pallas_call | solution.py:240
  87.3 3.6 %collective-permute-start.9 = (bf16[2,128,512]{2,1,0:T(8,128)(2,1)}, bf16[2,128,512]{2,1,0:T(8,128)(2,1)S(1)}, u32[]{:S(2)}, u32[]{:S(2)}) collective-permute-start(bf16[2,128,512]{2,1,0:T(8,128)(2,1)} %get-tuple-element.67), channel_id=1, source_target_pairs={{8,0},{16,8},{24,16},{9,1},{17,9},{25,17},{10,2},{18,10},{26,18},{... | collective-permute-start | bytes 786440 | tf_op jit(solution)/shard_map/ppermute | solution.py:23
  91.0 2.3 %collective-permute-done.8 = bf16[2,128,512]{2,1,0:T(8,128)(2,1)S(1)} collective-permute-done((bf16[2,128,512]{2,1,0:T(8,128)(2,1)}, bf16[2,128,512]{2,1,0:T(8,128)(2,1)S(1)}, u32[]{:S(2)}, u32[]{:S(2)}) %collective-permute-start.8) | collective-permute-done | bytes 262176 | tf_op jit(solution)/shard_map/ppermute | solution.py:23
  95.2 1.9 %fusion = f32[2,256,512]{2,1,0:T(8,128)} fusion(f32[2,256,512]{2,1,0:T(8,128)} %add_dynamic-update-slice_fusion, bf16[2,128,512]{2,1,0:T(8,128)(2,1)S(1)} %collective-permute-done.9), kind=kLoop, calls=%fused_computation.1 | loop fusion | flops 262144 | bytes 1310720 | tf_op jit(solution)/shard_map/scatter-add | solution.py:370
  98.6 3.4 %collective-permute-start.10 = (bf16[2,256,128]{2,1,0:T(8,128)(2,1)S(1)}, bf16[2,256,128]{2,1,0:T(8,128)(2,1)S(1)}, u32[]{:S(2)}, u32[]{:S(2)}) collective-permute-start(bf16[2,256,128]{2,1,0:T(8,128)(2,1)S(1)} %get-tuple-element.73), channel_id=1, source_target_pairs={{0,1},{1,2},{2,3},{3,4},{4,5},{5,6},{6,7},{8,9},{9,10},{10,11},{11... | collective-permute-start | bytes 393224 | tf_op jit(solution)/shard_map/ppermute | solution.py:23
  102.0 3.4 %collective-permute-start.11 = (bf16[2,256,128]{2,1,0:T(8,128)(2,1)S(1)}, bf16[2,256,128]{2,1,0:T(8,128)(2,1)S(1)}, u32[]{:S(2)}, u32[]{:S(2)}) collective-permute-start(bf16[2,256,128]{2,1,0:T(8,128)(2,1)S(1)} %get-tuple-element.72), channel_id=1, source_target_pairs={{1,0},{2,1},{3,2},{4,3},{5,4},{6,5},{7,6},{9,8},{10,9},{11,10},{12... | collective-permute-start | bytes 393224 | tf_op jit(solution)/shard_map/ppermute | solution.py:23
  105.4 5.1 %all-to-all-start.2 = ((bf16[8,1,2,32,256]{4,3,2,1,0:T(8,128)(2,1)}), bf16[8,1,2,32,256]{4,3,2,1,0:T(8,128)(2,1)S(1)}, u32[]{:S(2)}, u32[]{:S(2)}) async-start(bf16[8,1,2,32,256]{4,3,2,1,0:T(8,128)(2,1)} %get-tuple-element.68), calls=%async_computation.2 | async-start | bytes 524288 | tf_op jit(solution)/shard_map/all_to_all | solution.py:350
  110.6 5.3 %mode_sums.1 = (f32[12,2,32,256]{3,2,1,0:T(8,128)}, bf16[12,2,32,256]{3,2,1,0:T(8,128)(2,1)}) custom-call(f32[8,128]{1,0:T(8,128)} %add.45.weights, bf16[8,3,2,32,256]{4,3,2,1,0:T(8,128)(2,1)} %copy-done.2), custom_call_target="tpu_custom_call" | custom-call | tf_op jit(solution)/shard_map/mode_sums/pallas_call | solution.py:282
  118.0 7.2 %collective-permute-done.12.passed = bf16[12,2,32,256]{3,2,1,0:T(8,128)(2,1)S(1)} collective-permute-done((bf16[12,2,32,256]{3,2,1,0:T(8,128)(2,1)}, bf16[12,2,32,256]{3,2,1,0:T(8,128)(2,1)S(1)}, u32[]{:S(2)}, u32[]{:S(2)}) %collective-permute-start.12) | collective-permute-done | bytes 393248 | tf_op jit(solution)/shard_map/ppermute | solution.py:23
  125.9 3.0 %last_sums.1 = f32[1,12,2,32,256]{4,3,2,1,0:T(8,128)} custom-call(f32[8,128]{1,0:T(8,128)} %add.45.weights, bf16[8,1,2,32,256]{4,3,2,1,0:T(8,128)(2,1)} %copy-done.6, f32[12,2,32,256]{3,2,1,0:T(8,128)} %get-tuple-element.70.own, bf16[12,2,32,256]{3,2,1,0:T(8,128)(2,1)} %copy-done.11), custom_call_target="tpu_custom_call" | custom-call | tf_op jit(solution)/shard_map/last_sums/pallas_call | solution.py:313
  (74 shorter events, 24.7 us)
Async XLA Ops:
  2.4 3.6 %collective-permute-start = (f32[8,128]{1,0:T(8,128)S(1)}, f32[8,128]{1,0:T(8,128)S(1)}, u32[]{:S(2)}, u32[]{:S(2)}) collective-permute-start(f32[8,128]{1,0:T(8,128)S(1)} %broadcast_select_fusion), channel_id=1, source_target_pairs={{0,1},{1,0},{2,3},{3,2},{4,5},{5,4},{6,7},{7,6},{8,9},{9,8},{10,11... | collective-permute-start | bytes 12296 | tf_op jit(solution)/shard_map/ppermute | solution.py:46
  3.9 11.0 %collective-permute-start.3 = (bf16[1,12,2,32,256]{4,3,2,1,0:T(8,128)(2,1)}, bf16[1,12,2,32,256]{4,3,2,1,0:T(8,128)(2,1)S(1)}, u32[]{:S(2)}, u32[]{:S(2)}) collective-permute-start(bf16[1,12,2,32,256]{4,3,2,1,0:T(8,128)(2,1)} %own.3), channel_id=1, source_target_pairs={{8,0},{16,8},{24,16},{9,1},{17,9},{25,17},{10,2},{18,10},{26,18},{... | collective-permute-start | bytes 1179656 | tf_op jit(solution)/shard_map/ppermute | solution.py:23
  6.1 3.6 %collective-permute-start.1 = (f32[8,128]{1,0:T(8,128)S(1)}, f32[8,128]{1,0:T(8,128)S(1)}, u32[]{:S(2)}, u32[]{:S(2)}) collective-permute-start(f32[8,128]{1,0:T(8,128)S(1)} %fusion.3), channel_id=1, source_target_pairs={{0,2},{1,3},{2,0},{3,1},{4,6},{5,7},{6,4},{7,5},{8,10},{9,11},{10,... | collective-permute-start | bytes 12296 | tf_op jit(solution)/shard_map/ppermute | solution.py:46
  9.7 4.5 %collective-permute-start.2 = (f32[8,128]{1,0:T(8,128)S(1)}, f32[8,128]{1,0:T(8,128)S(1)}, u32[]{:S(2)}, u32[]{:S(2)}) collective-permute-start(f32[8,128]{1,0:T(8,128)S(1)} %fusion.12), channel_id=1, source_target_pairs={{0,4},{1,5},{2,6},{3,7},{4,0},{5,1},{6,2},{7,3},{8,12},{9,13},{10,... | collective-permute-start | bytes 12296 | tf_op jit(solution)/shard_map/ppermute | solution.py:46
  14.8 10.4 %copy-start.9 = (f32[2,256,256]{2,1,0:T(8,128)S(1)}, f32[2,256,256]{2,1,0:T(8,128)}, u32[]{:S(2)}) copy-start(f32[2,256,256]{2,1,0:T(8,128)} %param.17) | copy-start | bytes 1572868
  19.1 24.9 %all-to-all-start = ((bf16[8,3,2,32,256]{4,3,2,1,0:T(8,128)(2,1)}), bf16[8,3,2,32,256]{4,3,2,1,0:T(8,128)(2,1)S(1)}, u32[]{:S(2)}, u32[]{:S(2)}) async-start(bf16[8,3,2,32,256]{4,3,2,1,0:T(8,128)(2,1)} %slabs.2), calls=%async_computation | async-start | bytes 1572864 | tf_op jit(solution)/shard_map/all_to_all | solution.py:350
  25.2 23.2 %copy-start.1 = (bf16[2,256,256]{2,1,0:T(8,128)(2,1)}, bf16[2,256,256]{2,1,0:T(8,128)(2,1)S(1)}, u32[]{:S(2)}) copy-start(bf16[2,256,256]{2,1,0:T(8,128)(2,1)S(1)} %convert_element_type.39.tile) | copy-start | bytes 786436
  25.3 18.7 %collective-permute-start.4 = (bf16[2,256,128]{2,1,0:T(8,128)(2,1)S(1)}, bf16[2,256,128]{2,1,0:T(8,128)(2,1)S(1)}, u32[]{:S(2)}, u32[]{:S(2)}) collective-permute-start(bf16[2,256,128]{2,1,0:T(8,128)(2,1)S(1)} %get-tuple-element.77), channel_id=1, source_target_pairs={{0,1},{1,2},{2,3},{3,4},{4,5},{5,6},{6,7},{8,9},{9,10},{10,11},{11... | collective-permute-start | bytes 393224 | tf_op jit(solution)/shard_map/ppermute | solution.py:23
  28.7 25.3 %copy-start.14 = (s32[1,1,4,2]{2,3,1,0:T(2,128)S(1)}, s32[1,1,4,2]{2,3,1,0:T(2,128)}, u32[]{:S(2)}) copy-start(s32[1,1,4,2]{2,3,1,0:T(2,128)} %param.20) | copy-start | bytes 100
  28.7 13.5 %collective-permute-start.5 = (bf16[2,256,128]{2,1,0:T(8,128)(2,1)S(1)}, bf16[2,256,128]{2,1,0:T(8,128)(2,1)S(1)}, u32[]{:S(2)}, u32[]{:S(2)}) collective-permute-start(bf16[2,256,128]{2,1,0:T(8,128)(2,1)S(1)} %get-tuple-element.76), channel_id=1, source_target_pairs={{1,0},{2,1},{3,2},{4,3},{5,4},{6,5},{7,6},{9,8},{10,9},{11,10},{12... | collective-permute-start | bytes 393224 | tf_op jit(solution)/shard_map/ppermute | solution.py:23
  42.2 15.7 %copy-start.8 = (bf16[2,256,128]{2,1,0:T(8,128)(2,1)}, bf16[2,256,128]{2,1,0:T(8,128)(2,1)S(1)}, u32[]{:S(2)}) copy-start(bf16[2,256,128]{2,1,0:T(8,128)(2,1)S(1)} %collective-permute-done.5.right) | copy-start | bytes 393220
  44.0 13.9 %copy-start.7 = (bf16[2,256,128]{2,1,0:T(8,128)(2,1)}, bf16[2,256,128]{2,1,0:T(8,128)(2,1)S(1)}, u32[]{:S(2)}) copy-start(bf16[2,256,128]{2,1,0:T(8,128)(2,1)S(1)} %collective-permute-done.4.left) | copy-start | bytes 393220
  44.0 19.2 %copy-start.3 = (bf16[8,3,2,32,256]{4,3,2,1,0:T(8,128)(2,1)}, bf16[8,3,2,32,256]{4,3,2,1,0:T(8,128)(2,1)S(1)}, u32[]{:S(2)}) copy-start(bf16[8,3,2,32,256]{4,3,2,1,0:T(8,128)(2,1)S(1)} %all-to-all-done.probes) | copy-start | bytes 2359300
  44.0 26.2 %all-to-all-start.1 = ((bf16[8,1,2,32,256]{4,3,2,1,0:T(8,128)(2,1)}), bf16[8,1,2,32,256]{4,3,2,1,0:T(8,128)(2,1)S(1)}, u32[]{:S(2)}, u32[]{:S(2)}) async-start(bf16[8,1,2,32,256]{4,3,2,1,0:T(8,128)(2,1)} %slabs.3), calls=%async_computation.1 | async-start | bytes 524288 | tf_op jit(solution)/shard_map/all_to_all | solution.py:350
  48.4 7.7 %collective-permute-start.6 = (bf16[2,128,512]{2,1,0:T(8,128)(2,1)S(1)}, bf16[2,128,512]{2,1,0:T(8,128)(2,1)S(1)}, u32[]{:S(2)}, u32[]{:S(2)}) collective-permute-start(bf16[2,128,512]{2,1,0:T(8,128)(2,1)S(1)} %pad_maximum_fusion), channel_id=1, source_target_pairs={{0,8},{8,16},{16,24},{1,9},{9,17},{17,25},{2,10},{10,18},{18,26},{... | collective-permute-start | bytes 786440 | tf_op jit(solution)/shard_map/ppermute | solution.py:23
  50.4 7.5 %collective-permute-start.7 = (bf16[2,128,512]{2,1,0:T(8,128)(2,1)S(1)}, bf16[2,128,512]{2,1,0:T(8,128)(2,1)S(1)}, u32[]{:S(2)}, u32[]{:S(2)}) collective-permute-start(bf16[2,128,512]{2,1,0:T(8,128)(2,1)S(1)} %pad_maximum_fusion.1), channel_id=1, source_target_pairs={{8,0},{16,8},{24,16},{9,1},{17,9},{25,17},{10,2},{18,10},{26,18},{... | collective-permute-start | bytes 786440 | tf_op jit(solution)/shard_map/ppermute | solution.py:23
  70.2 35.2 %all-to-all-start.3 = ((bf16[8,3,2,32,256]{4,3,2,1,0:T(8,128)(2,1)}), bf16[8,3,2,32,256]{4,3,2,1,0:T(8,128)(2,1)S(1)}, u32[]{:S(2)}, u32[]{:S(2)}) async-start(bf16[8,3,2,32,256]{4,3,2,1,0:T(8,128)(2,1)} %get-tuple-element.69), calls=%async_computation.3 | async-start | bytes 1572864 | tf_op jit(solution)/shard_map/all_to_all | solution.py:350
  85.4 7.9 %collective-permute-start.8 = (bf16[2,128,512]{2,1,0:T(8,128)(2,1)}, bf16[2,128,512]{2,1,0:T(8,128)(2,1)S(1)}, u32[]{:S(2)}, u32[]{:S(2)}) collective-permute-start(bf16[2,128,512]{2,1,0:T(8,128)(2,1)} %get-tuple-element.66), channel_id=1, source_target_pairs={{0,8},{8,16},{16,24},{1,9},{9,17},{17,25},{2,10},{10,18},{18,26},{... | collective-permute-start | bytes 786440 | tf_op jit(solution)/shard_map/ppermute | solution.py:23
  87.3 7.9 %collective-permute-start.9 = (bf16[2,128,512]{2,1,0:T(8,128)(2,1)}, bf16[2,128,512]{2,1,0:T(8,128)(2,1)S(1)}, u32[]{:S(2)}, u32[]{:S(2)}) collective-permute-start(bf16[2,128,512]{2,1,0:T(8,128)(2,1)} %get-tuple-element.67), channel_id=1, source_target_pairs={{8,0},{16,8},{24,16},{9,1},{17,9},{25,17},{10,2},{18,10},{26,18},{... | collective-permute-start | bytes 786440 | tf_op jit(solution)/shard_map/ppermute | solution.py:23
  98.6 19.2 %collective-permute-start.10 = (bf16[2,256,128]{2,1,0:T(8,128)(2,1)S(1)}, bf16[2,256,128]{2,1,0:T(8,128)(2,1)S(1)}, u32[]{:S(2)}, u32[]{:S(2)}) collective-permute-start(bf16[2,256,128]{2,1,0:T(8,128)(2,1)S(1)} %get-tuple-element.73), channel_id=1, source_target_pairs={{0,1},{1,2},{2,3},{3,4},{4,5},{5,6},{6,7},{8,9},{9,10},{10,11},{11... | collective-permute-start | bytes 393224 | tf_op jit(solution)/shard_map/ppermute | solution.py:23
  102.0 15.8 %collective-permute-start.11 = (bf16[2,256,128]{2,1,0:T(8,128)(2,1)S(1)}, bf16[2,256,128]{2,1,0:T(8,128)(2,1)S(1)}, u32[]{:S(2)}, u32[]{:S(2)}) collective-permute-start(bf16[2,256,128]{2,1,0:T(8,128)(2,1)S(1)} %get-tuple-element.72), channel_id=1, source_target_pairs={{1,0},{2,1},{3,2},{4,3},{5,4},{6,5},{7,6},{9,8},{10,9},{11,10},{12... | collective-permute-start | bytes 393224 | tf_op jit(solution)/shard_map/ppermute | solution.py:23
  105.4 12.5 %all-to-all-start.2 = ((bf16[8,1,2,32,256]{4,3,2,1,0:T(8,128)(2,1)}), bf16[8,1,2,32,256]{4,3,2,1,0:T(8,128)(2,1)S(1)}, u32[]{:S(2)}, u32[]{:S(2)}) async-start(bf16[8,1,2,32,256]{4,3,2,1,0:T(8,128)(2,1)} %get-tuple-element.68), calls=%async_computation.2 | async-start | bytes 524288 | tf_op jit(solution)/shard_map/all_to_all | solution.py:350
  115.9 9.3 %collective-permute-start.12 = (bf16[12,2,32,256]{3,2,1,0:T(8,128)(2,1)}, bf16[12,2,32,256]{3,2,1,0:T(8,128)(2,1)S(1)}, u32[]{:S(2)}, u32[]{:S(2)}) collective-permute-start(bf16[12,2,32,256]{3,2,1,0:T(8,128)(2,1)} %get-tuple-element.71), channel_id=1, source_target_pairs={{0,8},{8,16},{16,24},{1,9},{9,17},{17,25},{2,10},{10,18},{18,26},{... | collective-permute-start | bytes 1179656 | tf_op jit(solution)/shard_map/ppermute | solution.py:23
  117.9 11.0 %copy-start.4 = (f32[2,256,256]{2,1,0:T(8,128)}, f32[2,256,256]{2,1,0:T(8,128)S(1)}, u32[]{:S(2)}) copy-start(f32[2,256,256]{2,1,0:T(8,128)S(1)} %fusion.1) | copy-start | bytes 1572868
  (8 other events, 27.2 us)
